TPU v7x, 32 devices: a whole 2x2x4 slice. The times are simulated.
32 devices in a mesh: grp: 2 (over x), pool: 16 (over z, y, core).
Axes of the slice: x: 2, y: 2, z: 4, core: 2. Of those that a mesh axis runs over, the one named last changes fastest.
Arguments:
- queries: bfloat16 [32, 128, 1024], P(('grp', 'pool')), parts along dimension 0, may hold values from -400 to 400
- new_kv: bfloat16 [32, 128, 256], P(('grp', 'pool')), parts along dimension 0, may hold values from -16 to 16
- pool_kv: bfloat16 [64, 8, 128, 256], P(('grp', 'pool')), parts along dimension 0, may hold values from -16 to 16
- hit_slots: int32 [4, 16], P('grp'), parts along dimension 0, may hold values from 0 to 31, as said below
- prefix_blocks: int32 [4], P('grp'), parts along dimension 0, may hold values from 1 to 16, 20 in all
- new_owners: int32 [4, 2], P('grp'), parts along dimension 0, may hold values from 0 to 15, as said below
Outputs:
- attended: bfloat16 [32, 128, 1024], P(('grp', 'pool')), parts along dimension 0
- new_store: bfloat16 [32, 8, 128, 256], P(('grp', 'pool')), parts along dimension 0
There are 2 independent parts, one for each index of `grp`. A program takes and returns all parts, laid end to end along the dimension named above; each array names one. Nothing has to cross between parts.
Inputs may be any that keep to these rules, and one draw needn't show every extreme that they name: `hit_slots`: slot s lies on owner s // 2. Block j of request r lies on owner (f + j) mod 16, where f depends on r and is a multiple of 4; one owner keeps different requests in different slots. Entries with j >= prefix_blocks[r] are unused. `prefix_blocks`: they sum to 20. `new_owners`: all 4 entries are distinct.
All inputs are finite; a program needn't handle non-finite values.
Results may differ from a plain program's by a relative error of at most 0.009.
Values may be sent and summed in bfloat16 or wider, within the bound.
No kernel may reach another device: no remote copies, remote signals or barrier semaphores. Data moves between devices by JAX's collectives and lax.ppermute only.
A program may use at most 64 MiB of HBM per device.

v0:
```python
import math
import jax
import jax.numpy as jnp
from jax import lax
from jax.sharding import PartitionSpec as P

group_slots = 4
minus_big = -1e30


def fold_keys(state_now, query_rows, key_rows, values, usable, score_scale):
    maximum, totals, accumulated = state_now
    scores = (
        jnp.einsum("tgd,kd->tgk", query_rows, key_rows, preferred_element_type=jnp.float32)
        * score_scale
    )
    scores = jnp.where(usable, scores, minus_big)
    maximum_new = jnp.maximum(maximum, jnp.max(scores, axis=2))
    weights = jnp.where(usable, jnp.exp(scores - maximum_new[:, :, None]), 0.0)
    factor = jnp.exp(maximum - maximum_new)
    totals = totals * factor + jnp.sum(weights, axis=2)
    accumulated = accumulated * factor[:, :, None] + jnp.einsum(
        "tgk,kd->tgd", weights.astype(jnp.bfloat16), values, preferred_element_type=jnp.float32
    )
    return (maximum_new, totals, accumulated)


def attend_blocks(state_now, query_rows, stored, first_slot, live_count, score_scale):
    slot_total = stored.shape[0]
    block_len = stored.shape[1]
    row_width = stored.shape[2]
    head_dim = row_width // 2
    loop_steps = (live_count + group_slots - 1) // group_slots
    offsets = jnp.arange(group_slots * block_len, dtype=jnp.int32) // block_len

    def advance(turn_index, state_in):
        start_slot = (first_slot + turn_index * group_slots) % slot_total
        block_rows = lax.dynamic_slice_in_dim(stored, start_slot, group_slots, 0).reshape(
            group_slots * block_len, row_width
        )
        usable = (turn_index * group_slots + offsets < live_count)[None, None, :]
        return fold_keys(
            state_in,
            query_rows,
            block_rows[:, :head_dim],
            block_rows[:, head_dim:],
            usable,
            score_scale,
        )

    return lax.fori_loop(0, loop_steps, advance, state_now)


def on_device(queries, new_kv, pool_kv, hit_slots, prefix_blocks, new_owners):
    my_index = lax.axis_index("pool")
    slot_count = pool_kv.shape[0]
    kv_heads = pool_kv.shape[1]
    block_len = pool_kv.shape[2]
    row_width = pool_kv.shape[3]
    head_dim = row_width // 2
    requests = hit_slots.shape[0]
    longest = hit_slots.shape[1]
    groups = queries.shape[2] // head_dim
    score_scale = 1.0 / math.sqrt(head_dim)
    request = my_index // kv_heads
    positions = jnp.arange(longest, dtype=jnp.int32)
    is_live = positions[None, :] < prefix_blocks[:, None]
    on_me = (hit_slots // slot_count == my_index) & is_live
    holds_block = jnp.any(on_me, axis=1)
    local_slot = jnp.sum(jnp.where(on_me, hit_slots % slot_count, 0), axis=1)
    picked = jnp.take(pool_kv, local_slot, axis=0)
    outgoing = jnp.where(holds_block[:, None, None, None], picked, jnp.zeros_like(picked))
    outgoing = outgoing.reshape(requests * kv_heads, block_len, row_width)
    fetched = lax.all_to_all(outgoing, "pool", split_axis=0, concat_axis=0, tiled=True)
    query_rows = queries[0].reshape(block_len, groups, head_dim)
    own_new = new_kv[0]
    causal = (jnp.arange(block_len)[None, :] <= jnp.arange(block_len)[:, None])[:, None, :]
    empty_state = (
        jnp.full((block_len, groups), minus_big, jnp.float32),
        jnp.zeros((block_len, groups), jnp.float32),
        jnp.zeros((block_len, groups, head_dim), jnp.float32),
    )
    state_now = fold_keys(
        empty_state, query_rows, own_new[:, :head_dim], own_new[:, head_dim:], causal, score_scale
    )
    own_length = prefix_blocks[request]
    own_first = hit_slots[request, 0] // slot_count
    state_now = attend_blocks(state_now, query_rows, fetched, own_first, own_length, score_scale)
    attended = (
        (state_now[2] / state_now[1][:, :, None])
        .reshape(block_len, groups * head_dim)
        .astype(jnp.bfloat16)[None]
    )
    arrived = lax.all_gather(new_kv, "pool", axis=0, tiled=True)
    owned_by_me = jnp.any(new_owners == my_index, axis=1)
    source_request = jnp.sum(jnp.where(owned_by_me, jnp.arange(requests, dtype=jnp.int32), 0))
    owned = jnp.any(owned_by_me)
    new_block = lax.dynamic_slice_in_dim(arrived, source_request * kv_heads, kv_heads, 0)
    new_store = jnp.where(owned, new_block, jnp.zeros_like(new_block))[None]
    return (attended, new_store)


def solution(mesh):
    placed = (
        P(("grp", "pool"), None, None),
        P(("grp", "pool"), None, None),
        P(("grp", "pool"), None, None, None),
        P("grp", None),
        P("grp"),
        P("grp", None),
    )
    return jax.shard_map(
        on_device,
        mesh=mesh,
        in_specs=placed,
        out_specs=(P(("grp", "pool"), None, None), P(("grp", "pool"), None, None, None)),
        check_vma=False,
    )
```

profile of v0, /device:TPU:0, one launch (start us, length us, event | category | flops | bytes accessed | tf_op | source)
XLA Modules:
  0.0 74.9 jit_solution(3903400085508740048)
XLA Ops:
  7.2 1.0 %fusion.36 = (pred[2]{0:T(512)(128)(4,1)S(1)}, pred[2,16]{1,0:T(4,128)(4,1)S(1)}) fusion(s32[2]{0:T(128)} %param.12, s32[]{:T(128)S(6)} %axis_index.12, s32[2,16]{1,0:T(2,128)} %param.11), kind=kLoop, calls=%fused_computation.73 | loop fusion | flops 606 | bytes 174 | tf_op jit(solution)/shard_map/reduce_or | solution.py:69
  8.2 0.8 %fusion.30 = s32[2]{0:T(128)S(1)} fusion(pred[2,16]{1,0:T(4,128)(4,1)S(1)} %get-tuple-element.196, s32[2,16]{1,0:T(2,128)} %param.11), kind=kLoop, calls=%fused_computation.62 | loop fusion | flops 414 | bytes 168 | tf_op jit(solution)/shard_map/reduce_sum | solution.py:70
  9.3 0.6 gather_fusion
  10.0 1.3 %fusion.22 = bf16[16,128,256]{2,1,0:T(8,128)(2,1)} fusion(bf16[2,8,128,256]{3,2,1,0:T(8,128)(2,1)S(1)} %gather_fusion, pred[16]{0:T(512)(128)(4,1)S(1)} %broadcast_in_dim.118, pred[16]{0:T(512)(128)(4,1)S(1)} %broadcast_in_dim.115), kind=kLoop, calls=%fused_computation.37 | loop fusion | flops 1048576 | bytes 2097184 | tf_op jit(solution)/shard_map/jit(_where)/select_n | solution.py:72
  11.3 7.5 %all-to-all-start = ((bf16[16,128,256]{2,1,0:T(8,128)(2,1)}), bf16[16,128,256]{2,1,0:T(8,128)(2,1)S(1)}, u32[]{:S(2)}, u32[]{:S(2)}) async-start(bf16[16,128,256]{2,1,0:T(8,128)(2,1)} %fusion.22), calls=%async_computation | async-start | bytes 2097152 | tf_op jit(solution)/shard_map/all_to_all | solution.py:74
  18.9 0.7 all-gather.2.cloned.1.call-update
  19.6 0.5 constant_dynamic-slice_fusion.1
  22.7 0.6 dynamic_slice.15
  24.2 0.2 copy.21
  24.4 0.7 fusion.34
  25.0 0.7 select_reduce_fusion
  26.4 0.2 fusion.37
  26.7 0.3 convolution_add_fusion.1
  27.1 15.8 %all-to-all-done = bf16[16,128,256]{2,1,0:T(8,128)(2,1)S(1)} async-done(((bf16[16,128,256]{2,1,0:T(8,128)(2,1)}), bf16[16,128,256]{2,1,0:T(8,128)(2,1)S(1)}, u32[]{:S(2)}, u32[]{:S(2)}) %all-to-all-start) | async-done | bytes 1048608 | tf_op jit(solution)/shard_map/all_to_all | solution.py:74
  42.8 2.8 %while.17 = (s32[]{:T(128)}, f32[128,8]{0,1:T(8,128)S(1)}, f32[128,8]{0,1:T(8,128)S(1)}, f32[128,8,128]{2,0,1:T(8,128)S(1)}, s32[]{:T(128)}, /*index=5*/s32[]{:T...) while((s32[]{:T(128)}, f32[128,8]{0,1:T(8,128)S(1)}, ...), condition=%wide.region_7.8_spmd.clone, body=%wide.region_4.7_spmd.clone.sunk | while | flops 275520512 | bytes 8457016 | solution.py:51
  42.8 0.7 fusion.46
  43.5 0.5 bitcast_reduce_fusion.2
  44.0 0.6 fusion.47
  44.6 1.0 %convolution_add_fusion.3 = f32[128,8,128]{2,0,1:T(8,128)S(1)} fusion(f32[512,128,8]{1,0,2:T(8,128)S(1)} %get-tuple-element.264, f32[128,8]{0,1:T(8,128)S(1)} %max.8, pred[512]{0:T(512)(128)(4,1)S(1)} %fusion.46, f32[128,8,128]{2,0,1:T(8,128)S(1)} %get-tuple-element.284, f32[128,8]{0,1:T(8,128)S(1)} %get-tuple-element.266, ...), kind=kOutput, calls=%fused_computation.9.clone.1 | convolution fusion | flops 137101312 | bytes 3286016 | tf_op jit(solution)/shard_map/while/body/tgk,kd->tgd/dot_general | solution.py:22
  45.6 0.2 divide_convert_fusion
  45.9 0.2 copy.22
  46.0 0.8 %convert_element_type.24 = bf16[1,128,1024]{2,1,0:T(8,128)(2,1)} reshape(bf16[128,8,128]{2,1,0:T(8,128)(2,1)S(1)} %copy.22) | data formatting | bytes 524288 | tf_op jit(solution)/shard_map/convert_element_type | solution.py:92
  46.9 18.7 %all-gather.2.cloned.1.call-done = bf16[16,128,256]{2,1,0:T(8,128)(2,1)} async-done(((bf16[1,128,256]{2,1,0:T(8,128)(2,1)}), bf16[16,128,256]{2,1,0:T(8,128)(2,1)}) %all-gather.2.cloned.1.call-update) | async-done | bytes 1048592 | tf_op jit(solution)/shard_map/all_gather | solution.py:94
  65.6 2.5 %select_bitcast_fusion = bf16[1,8,128,256]{3,2,1,0:T(8,128)(2,1)} fusion(bf16[16,128,256]{2,1,0:T(8,128)(2,1)} %all-gather.2.cloned.1.call-done, s32[]{:T(128)S(6)} %select_n.133, pred[]{:T(512)} %get-tuple-element.173), kind=kLoop, calls=%fused_computation.38 | loop fusion | flops 262144 | bytes 1048581 | tf_op jit(solution)/shard_map/broadcast_in_dim | solution.py:99
  (29 shorter events, 0.8 us)
Async XLA Ops:
  7.2 2.1 %copy-start = (bf16[2,8,128,256]{3,2,1,0:T(8,128)(2,1)S(1)}, bf16[2,8,128,256]{3,2,1,0:T(8,128)(2,1)}, u32[]{:S(2)}) copy-start(bf16[2,8,128,256]{3,2,1,0:T(8,128)(2,1)} %param.10) | copy-start | bytes 3145732
  9.9 9.6 %copy-start.3 = (s32[2,16]{1,0:T(2,128)S(1)}, s32[2,16]{1,0:T(2,128)}, u32[]{:S(2)}) copy-start(s32[2,16]{1,0:T(2,128)} %param.11) | copy-start | bytes 388
  9.9 12.8 %copy-start.5 = (s32[2]{0:T(128)S(1)}, s32[2]{0:T(128)}, u32[]{:S(2)}) copy-start(s32[2]{0:T(128)} %param.12) | copy-start | bytes 28
  10.0 14.0 %copy-start.2 = (bf16[1,128,1024]{2,1,0:T(8,128)(2,1)S(1)}, bf16[1,128,1024]{2,1,0:T(8,128)(2,1)}, u32[]{:S(2)}) copy-start(bf16[1,128,1024]{2,1,0:T(8,128)(2,1)} %param.8) | copy-start | bytes 786436
  11.3 13.1 %copy-start.4 = (s32[2,2]{1,0:T(2,128)S(1)}, s32[2,2]{1,0:T(2,128)}, u32[]{:S(2)}) copy-start(s32[2,2]{1,0:T(2,128)} %param.13) | copy-start | bytes 52
  11.3 15.1 %copy-start.1 = (bf16[1,128,256]{2,1,0:T(8,128)(2,1)S(1)}, bf16[1,128,256]{2,1,0:T(8,128)(2,1)}, u32[]{:S(2)}) copy-start(bf16[1,128,256]{2,1,0:T(8,128)(2,1)} %param.9) | copy-start | bytes 196612
  11.3 31.6 %all-to-all-start = ((bf16[16,128,256]{2,1,0:T(8,128)(2,1)}), bf16[16,128,256]{2,1,0:T(8,128)(2,1)S(1)}, u32[]{:S(2)}, u32[]{:S(2)}) async-start(bf16[16,128,256]{2,1,0:T(8,128)(2,1)} %fusion.22), calls=%async_computation | async-start | bytes 2097152 | tf_op jit(solution)/shard_map/all_to_all | solution.py:74
  18.8 46.8 %all-gather.2.cloned.1.call-start = ((), (), s32[]{:S(2)}) async-start(), calls=%async_computation.1 | async-start | bytes 1114112 | tf_op jit(solution)/shard_map/all_gather | solution.py:94
Sparse Core Ops, SparseCore 0:
  21.8 43.7 all-gather.1
where the time goes:
time: 75.3 us; the launch traced here: 74.9 us
  waiting for transfers between devices  35.1 us (47%)
  between operations  18.1 us (24%)
  other arithmetic  8.52 us (11%)
  starting transfers between devices  7.59 us (10%)
  local copies, waits for them, and re-layouts  3.44 us (5%)
  matrix products  2.02 us (3%)
    all_gather x1, waiting for transfers between devices, on_device(): arrived = lax.all_gather(new_kv, 'pool', axis=0, tiled=True)  18.7 us
    all_to_all x1, waiting for transfers between devices, on_device(): lax.all_to_all(outgoing, 'pool', split_axis=0, concat_axis=0, tiled=True)  15.8 us
    all_to_all x1, starting transfers between devices, on_device(): lax.all_to_all(outgoing, 'pool', split_axis=0, concat_axis=0, tiled=True)  7.55 us
    broadcast_in_dim x1, other arithmetic, on_device(): new_store = jnp.where(owned, new_block, jnp.zeros_like(new_block))[None]  2.49 us
  transfers between devices with their start and end apart: 2, of which 2 were waited for; matrix products, arithmetic and copies ran while one was open for 10% of the time, Pallas kernels for 0%

commit v1 on v0

--- a/solution.py
+++ b/solution.py
@@ -91,7 +91,12 @@
         .reshape(block_len, groups * head_dim)
         .astype(jnp.bfloat16)[None]
     )
-    arrived = lax.all_gather(new_kv, "pool", axis=0, tiled=True)
+    ring = [new_kv]
+    for hop in range(15):
+        ring.append(lax.ppermute(ring[-1], "pool", [(dev, (dev + 1) % 16) for dev in range(16)]))
+    arrived = jnp.roll(
+        jnp.concatenate(ring[::-1], axis=0), (lax.axis_index("pool") + 1) * ring[0].shape[0], axis=0
+    )
     owned_by_me = jnp.any(new_owners == my_index, axis=1)
     source_request = jnp.sum(jnp.where(owned_by_me, jnp.arange(requests, dtype=jnp.int32), 0))
     owned = jnp.any(owned_by_me)

time: 75.3 us -> 142 us (1.89)
  the two profiles are of different devices: /device:TPU:0 before, /device:TPU:31 now
where the time goes in v1:
time: 142 us; the launch traced here: 141 us
  starting transfers between devices  72.3 us (51%)
  waiting for transfers between devices  31 us (22%)
  local copies, waits for them, and re-layouts  15.6 us (11%)
  other arithmetic  10.8 us (8%)
  matrix products  6.35 us (4%)
  between operations  4.63 us (3%)
    ppermute x15, starting transfers between devices, on_device(): lax.ppermute(ring[-1], 'pool', [(dev, (dev + 1) % 16) for dev in range(16)])  66.5 us
    ppermute x15, waiting for transfers between devices, on_device(): lax.ppermute(ring[-1], 'pool', [(dev, (dev + 1) % 16) for dev in range(16)])  31 us
    unnamed x69, local copies, waits for them, and re-layouts  12.4 us
    all_to_all x1, starting transfers between devices, on_device(): lax.all_to_all(outgoing, 'pool', split_axis=0, concat_axis=0, tiled=True)  5.87 us
    dot_general x5, matrix products, fold_keys(): jnp.einsum('tgk,kd->tgd', weights.astype(jnp.bfloat16), values, preferred...  4.3 us
  transfers between devices with their start and end apart: 16, of which 13 were waited for; matrix products, arithmetic and copies ran while one was open for 15% of the time, Pallas kernels for 0%

profile of v1, /device:TPU:31, one launch (start us, length us, event | category | flops | bytes accessed | tf_op | source)
XLA Modules:
  0.0 141.1 jit_solution(3429211989464040780)
XLA Ops:
  1.1 1.6 %collective-permute-done = bf16[1,128,256]{2,1,0:T(8,128)(2,1)S(1)} collective-permute-done((bf16[1,128,256]{2,1,0:T(8,128)(2,1)}, bf16[1,128,256]{2,1,0:T(8,128)(2,1)S(1)}, u32[]{:S(2)}, u32[]{:S(2)}) %collective-permute-start) | collective-permute-done | bytes 65568 | tf_op jit(solution)/shard_map/ppermute | solution.py:96
  2.8 5.0 %collective-permute-start.1 = (bf16[1,128,256]{2,1,0:T(8,128)(2,1)S(1)}, bf16[1,128,256]{2,1,0:T(8,128)(2,1)S(1)}, u32[]{:S(2)}, u32[]{:S(2)}) collective-permute-start(bf16[1,128,256]{2,1,0:T(8,128)(2,1)S(1)} %collective-permute-done), channel_id=1, source_target_pairs={{0,1},{1,2},{2,3},{3,4},{4,5},{5,6},{6,7},{7,8},{8,9},{9,10},{10,1... | collective-permute-start | bytes 196616 | tf_op jit(solution)/shard_map/ppermute | solution.py:96
  9.1 5.1 %collective-permute-start.2 = (bf16[1,128,256]{2,1,0:T(8,128)(2,1)S(1)}, bf16[1,128,256]{2,1,0:T(8,128)(2,1)S(1)}, u32[]{:S(2)}, u32[]{:S(2)}) collective-permute-start(bf16[1,128,256]{2,1,0:T(8,128)(2,1)S(1)} %collective-permute-done.1), channel_id=1, source_target_pairs={{0,1},{1,2},{2,3},{3,4},{4,5},{5,6},{6,7},{7,8},{8,9},{9,10},{10,1... | collective-permute-start | bytes 196616 | tf_op jit(solution)/shard_map/ppermute | solution.py:96
  15.5 5.1 %collective-permute-start.3 = (bf16[1,128,256]{2,1,0:T(8,128)(2,1)S(1)}, bf16[1,128,256]{2,1,0:T(8,128)(2,1)S(1)}, u32[]{:S(2)}, u32[]{:S(2)}) collective-permute-start(bf16[1,128,256]{2,1,0:T(8,128)(2,1)S(1)} %collective-permute-done.2), channel_id=1, source_target_pairs={{0,1},{1,2},{2,3},{3,4},{4,5},{5,6},{6,7},{7,8},{8,9},{9,10},{10,1... | collective-permute-start | bytes 196616 | tf_op jit(solution)/shard_map/ppermute | solution.py:96
  20.5 1.3 collective-permute-done.3
  21.9 5.1 %collective-permute-start.4 = (bf16[1,128,256]{2,1,0:T(8,128)(2,1)S(1)}, bf16[1,128,256]{2,1,0:T(8,128)(2,1)S(1)}, u32[]{:S(2)}, u32[]{:S(2)}) collective-permute-start(bf16[1,128,256]{2,1,0:T(8,128)(2,1)S(1)} %collective-permute-done.3), channel_id=1, source_target_pairs={{0,1},{1,2},{2,3},{3,4},{4,5},{5,6},{6,7},{7,8},{8,9},{9,10},{10,1... | collective-permute-start | bytes 196616 | tf_op jit(solution)/shard_map/ppermute | solution.py:96
  28.2 5.1 %collective-permute-start.5 = (bf16[1,128,256]{2,1,0:T(8,128)(2,1)S(1)}, bf16[1,128,256]{2,1,0:T(8,128)(2,1)S(1)}, u32[]{:S(2)}, u32[]{:S(2)}) collective-permute-start(bf16[1,128,256]{2,1,0:T(8,128)(2,1)S(1)} %collective-permute-done.4), channel_id=1, source_target_pairs={{0,1},{1,2},{2,3},{3,4},{4,5},{5,6},{6,7},{7,8},{8,9},{9,10},{10,1... | collective-permute-start | bytes 196616 | tf_op jit(solution)/shard_map/ppermute | solution.py:96
  34.6 5.1 %collective-permute-start.6 = (bf16[1,128,256]{2,1,0:T(8,128)(2,1)S(1)}, bf16[1,128,256]{2,1,0:T(8,128)(2,1)S(1)}, u32[]{:S(2)}, u32[]{:S(2)}) collective-permute-start(bf16[1,128,256]{2,1,0:T(8,128)(2,1)S(1)} %collective-permute-done.5), channel_id=1, source_target_pairs={{0,1},{1,2},{2,3},{3,4},{4,5},{5,6},{6,7},{7,8},{8,9},{9,10},{10,1... | collective-permute-start | bytes 196616 | tf_op jit(solution)/shard_map/ppermute | solution.py:96
  39.7 1.2 fusion.22
  40.9 5.9 %all-to-all-start = ((bf16[16,128,256]{2,1,0:T(8,128)(2,1)}), bf16[16,128,256]{2,1,0:T(8,128)(2,1)S(1)}, u32[]{:S(2)}, u32[]{:S(2)}) async-start(bf16[16,128,256]{2,1,0:T(8,128)(2,1)} %fusion.22), calls=%async_computation | async-start | bytes 2097152 | tf_op jit(solution)/shard_map/all_to_all | solution.py:74
  47.2 18.2 %collective-permute-done.7 = bf16[1,128,256]{2,1,0:T(8,128)(2,1)S(1)} collective-permute-done((bf16[1,128,256]{2,1,0:T(8,128)(2,1)S(1)}, bf16[1,128,256]{2,1,0:T(8,128)(2,1)S(1)}, u32[]{:S(2)}, u32[]{:S(2)}) %collective-permute-start.7) | collective-permute-done | bytes 65568 | tf_op jit(solution)/shard_map/ppermute | solution.py:96
  65.3 5.1 %collective-permute-start.8 = (bf16[1,128,256]{2,1,0:T(8,128)(2,1)S(1)}, bf16[1,128,256]{2,1,0:T(8,128)(2,1)S(1)}, u32[]{:S(2)}, u32[]{:S(2)}) collective-permute-start(bf16[1,128,256]{2,1,0:T(8,128)(2,1)S(1)} %collective-permute-done.7), channel_id=1, source_target_pairs={{0,1},{1,2},{2,3},{3,4},{4,5},{5,6},{6,7},{7,8},{8,9},{9,10},{10,1... | collective-permute-start | bytes 196616 | tf_op jit(solution)/shard_map/ppermute | solution.py:96
  71.8 5.1 %collective-permute-start.9 = (bf16[1,128,256]{2,1,0:T(8,128)(2,1)S(1)}, bf16[1,128,256]{2,1,0:T(8,128)(2,1)S(1)}, u32[]{:S(2)}, u32[]{:S(2)}) collective-permute-start(bf16[1,128,256]{2,1,0:T(8,128)(2,1)S(1)} %collective-permute-done.8), channel_id=1, source_target_pairs={{0,1},{1,2},{2,3},{3,4},{4,5},{5,6},{6,7},{7,8},{8,9},{9,10},{10,1... | collective-permute-start | bytes 196616 | tf_op jit(solution)/shard_map/ppermute | solution.py:96
  76.9 1.3 collective-permute-done.9
  78.2 5.1 %collective-permute-start.10 = (bf16[1,128,256]{2,1,0:T(8,128)(2,1)S(1)}, bf16[1,128,256]{2,1,0:T(8,128)(2,1)S(1)}, u32[]{:S(2)}, u32[]{:S(2)}) collective-permute-start(bf16[1,128,256]{2,1,0:T(8,128)(2,1)S(1)} %collective-permute-done.9), channel_id=1, source_target_pairs={{0,1},{1,2},{2,3},{3,4},{4,5},{5,6},{6,7},{7,8},{8,9},{9,10},{10,1... | collective-permute-start | bytes 196616 | tf_op jit(solution)/shard_map/ppermute | solution.py:96
  83.4 1.2 collective-permute-done.10
  84.6 5.1 %collective-permute-start.11 = (bf16[1,128,256]{2,1,0:T(8,128)(2,1)S(1)}, bf16[1,128,256]{2,1,0:T(8,128)(2,1)}, u32[]{:S(2)}, u32[]{:S(2)}) collective-permute-start(bf16[1,128,256]{2,1,0:T(8,128)(2,1)S(1)} %collective-permute-done.10), channel_id=1, source_target_pairs={{0,1},{1,2},{2,3},{3,4},{4,5},{5,6},{6,7},{7,8},{8,9},{9,10},{10,1... | collective-permute-start | bytes 196616 | tf_op jit(solution)/shard_map/ppermute | solution.py:96
  89.7 1.3 collective-permute-done.11
  91.0 5.2 %collective-permute-start.12 = (bf16[1,128,256]{2,1,0:T(8,128)(2,1)}, bf16[1,128,256]{2,1,0:T(8,128)(2,1)}, u32[]{:S(2)}, u32[]{:S(2)}) collective-permute-start(bf16[1,128,256]{2,1,0:T(8,128)(2,1)} %collective-permute-done.11), channel_id=1, source_target_pairs={{0,1},{1,2},{2,3},{3,4},{4,5},{5,6},{6,7},{7,8},{8,9},{9,10},{10,1... | collective-permute-start | bytes 196616 | tf_op jit(solution)/shard_map/ppermute | solution.py:96
  96.5 1.3 collective-permute-done.12
  97.8 5.1 %collective-permute-start.13 = (bf16[1,128,256]{2,1,0:T(8,128)(2,1)}, bf16[1,128,256]{2,1,0:T(8,128)(2,1)}, u32[]{:S(2)}, u32[]{:S(2)}) collective-permute-start(bf16[1,128,256]{2,1,0:T(8,128)(2,1)} %collective-permute-done.12), channel_id=1, source_target_pairs={{0,1},{1,2},{2,3},{3,4},{4,5},{5,6},{6,7},{7,8},{8,9},{9,10},{10,1... | collective-permute-start | bytes 196616 | tf_op jit(solution)/shard_map/ppermute | solution.py:96
  104.5 5.1 %collective-permute-start.14 = (bf16[1,128,256]{2,1,0:T(8,128)(2,1)}, bf16[1,128,256]{2,1,0:T(8,128)(2,1)}, u32[]{:S(2)}, u32[]{:S(2)}) collective-permute-start(bf16[1,128,256]{2,1,0:T(8,128)(2,1)} %collective-permute-done.13), channel_id=1, source_target_pairs={{0,1},{1,2},{2,3},{3,4},{4,5},{5,6},{6,7},{7,8},{8,9},{9,10},{10,1... | collective-permute-start | bytes 196616 | tf_op jit(solution)/shard_map/ppermute | solution.py:96
  127.4 1.5 %select_bitcast_fusion = bf16[1,8,128,256]{3,2,1,0:T(8,128)(2,1)} fusion(bf16[32,128,256]{2,1,0:T(8,128)(2,1)S(1)} %constant_dynamic-update-slice_fusion, s32[]{:T(128)S(6)} %dynamic_slice.22, pred[]{:T(512)} %get-tuple-element.164), kind=kLoop, calls=%fused_computation.38 | loop fusion | flops 262144 | bytes 1048581 | tf_op jit(solution)/shard_map/broadcast_in_dim | solution.py:104
  128.8 11.0 %while.17 = (s32[]{:T(128)}, f32[128,8]{0,1:T(8,128)S(1)}, f32[128,8]{0,1:T(8,128)S(1)}, f32[128,8,128]{2,0,1:T(8,128)S(1)}, s32[]{:T(128)}, /*index=5*/s32[]{:T...) while((s32[]{:T(128)}, f32[128,8]{0,1:T(8,128)S(1)}, ...), condition=%wide.region_7.8_spmd.clone, body=%wide.region_4.7_spmd.clone.sunk | while | flops 275520512 | bytes 8457016 | solution.py:51
  (136 shorter events, 35.4 us)
Async XLA Ops:
  0.6 32.7 %copy-start = (bf16[2,8,128,256]{3,2,1,0:T(8,128)(2,1)S(1)}, bf16[2,8,128,256]{3,2,1,0:T(8,128)(2,1)}, u32[]{:S(2)}) copy-start(bf16[2,8,128,256]{3,2,1,0:T(8,128)(2,1)} %param.10) | copy-start | bytes 3145732
  0.6 2.1 %collective-permute-start = (bf16[1,128,256]{2,1,0:T(8,128)(2,1)}, bf16[1,128,256]{2,1,0:T(8,128)(2,1)S(1)}, u32[]{:S(2)}, u32[]{:S(2)}) collective-permute-start(bf16[1,128,256]{2,1,0:T(8,128)(2,1)} %param.9), channel_id=1, source_target_pairs={{0,1},{1,2},{2,3},{3,4},{4,5},{5,6},{6,7},{7,8},{8,9},{9,10},{10,1... | collective-permute-start | bytes 196616 | tf_op jit(solution)/shard_map/ppermute | solution.py:96
  2.8 6.3 %collective-permute-start.1 = (bf16[1,128,256]{2,1,0:T(8,128)(2,1)S(1)}, bf16[1,128,256]{2,1,0:T(8,128)(2,1)S(1)}, u32[]{:S(2)}, u32[]{:S(2)}) collective-permute-start(bf16[1,128,256]{2,1,0:T(8,128)(2,1)S(1)} %collective-permute-done), channel_id=1, source_target_pairs={{0,1},{1,2},{2,3},{3,4},{4,5},{5,6},{6,7},{7,8},{8,9},{9,10},{10,1... | collective-permute-start | bytes 196616 | tf_op jit(solution)/shard_map/ppermute | solution.py:96
  9.1 6.4 %collective-permute-start.2 = (bf16[1,128,256]{2,1,0:T(8,128)(2,1)S(1)}, bf16[1,128,256]{2,1,0:T(8,128)(2,1)S(1)}, u32[]{:S(2)}, u32[]{:S(2)}) collective-permute-start(bf16[1,128,256]{2,1,0:T(8,128)(2,1)S(1)} %collective-permute-done.1), channel_id=1, source_target_pairs={{0,1},{1,2},{2,3},{3,4},{4,5},{5,6},{6,7},{7,8},{8,9},{9,10},{10,1... | collective-permute-start | bytes 196616 | tf_op jit(solution)/shard_map/ppermute | solution.py:96
  15.5 6.4 %collective-permute-start.3 = (bf16[1,128,256]{2,1,0:T(8,128)(2,1)S(1)}, bf16[1,128,256]{2,1,0:T(8,128)(2,1)S(1)}, u32[]{:S(2)}, u32[]{:S(2)}) collective-permute-start(bf16[1,128,256]{2,1,0:T(8,128)(2,1)S(1)} %collective-permute-done.2), channel_id=1, source_target_pairs={{0,1},{1,2},{2,3},{3,4},{4,5},{5,6},{6,7},{7,8},{8,9},{9,10},{10,1... | collective-permute-start | bytes 196616 | tf_op jit(solution)/shard_map/ppermute | solution.py:96
  21.9 6.4 %collective-permute-start.4 = (bf16[1,128,256]{2,1,0:T(8,128)(2,1)S(1)}, bf16[1,128,256]{2,1,0:T(8,128)(2,1)S(1)}, u32[]{:S(2)}, u32[]{:S(2)}) collective-permute-start(bf16[1,128,256]{2,1,0:T(8,128)(2,1)S(1)} %collective-permute-done.3), channel_id=1, source_target_pairs={{0,1},{1,2},{2,3},{3,4},{4,5},{5,6},{6,7},{7,8},{8,9},{9,10},{10,1... | collective-permute-start | bytes 196616 | tf_op jit(solution)/shard_map/ppermute | solution.py:96
  28.2 6.4 %collective-permute-start.5 = (bf16[1,128,256]{2,1,0:T(8,128)(2,1)S(1)}, bf16[1,128,256]{2,1,0:T(8,128)(2,1)S(1)}, u32[]{:S(2)}, u32[]{:S(2)}) collective-permute-start(bf16[1,128,256]{2,1,0:T(8,128)(2,1)S(1)} %collective-permute-done.4), channel_id=1, source_target_pairs={{0,1},{1,2},{2,3},{3,4},{4,5},{5,6},{6,7},{7,8},{8,9},{9,10},{10,1... | collective-permute-start | bytes 196616 | tf_op jit(solution)/shard_map/ppermute | solution.py:96
  33.9 36.5 %copy-start.1 = (bf16[1,128,256]{2,1,0:T(8,128)(2,1)S(1)}, bf16[1,128,256]{2,1,0:T(8,128)(2,1)}, u32[]{:S(2)}) copy-start(bf16[1,128,256]{2,1,0:T(8,128)(2,1)} %param.9) | copy-start | bytes 196612
  34.6 12.4 %collective-permute-start.6 = (bf16[1,128,256]{2,1,0:T(8,128)(2,1)S(1)}, bf16[1,128,256]{2,1,0:T(8,128)(2,1)S(1)}, u32[]{:S(2)}, u32[]{:S(2)}) collective-permute-start(bf16[1,128,256]{2,1,0:T(8,128)(2,1)S(1)} %collective-permute-done.5), channel_id=1, source_target_pairs={{0,1},{1,2},{2,3},{3,4},{4,5},{5,6},{6,7},{7,8},{8,9},{9,10},{10,1... | collective-permute-start | bytes 196616 | tf_op jit(solution)/shard_map/ppermute | solution.py:96
  40.9 61.9 %copy-start.16 = (s32[2,2]{1,0:T(2,128)S(1)}, s32[2,2]{1,0:T(2,128)}, u32[]{:S(2)}) copy-start(s32[2,2]{1,0:T(2,128)} %param.13) | copy-start | bytes 52
  40.9 69.9 %copy-start.15 = (s32[2,16]{1,0:T(2,128)S(1)}, s32[2,16]{1,0:T(2,128)}, u32[]{:S(2)}) copy-start(s32[2,16]{1,0:T(2,128)} %param.11) | copy-start | bytes 388
  40.9 87.9 %all-to-all-start = ((bf16[16,128,256]{2,1,0:T(8,128)(2,1)}), bf16[16,128,256]{2,1,0:T(8,128)(2,1)S(1)}, u32[]{:S(2)}, u32[]{:S(2)}) async-start(bf16[16,128,256]{2,1,0:T(8,128)(2,1)} %fusion.22), calls=%async_computation | async-start | bytes 2097152 | tf_op jit(solution)/shard_map/all_to_all | solution.py:74
  46.8 66.8 %copy-start.17 = (s32[2]{0:T(128)S(1)}, s32[2]{0:T(128)}, u32[]{:S(2)}) copy-start(s32[2]{0:T(128)} %param.12) | copy-start | bytes 28
  47.0 67.8 %copy-start.5 = (bf16[1,128,256]{2,1,0:T(8,128)(2,1)}, bf16[1,128,256]{2,1,0:T(8,128)(2,1)S(1)}, u32[]{:S(2)}) copy-start(bf16[1,128,256]{2,1,0:T(8,128)(2,1)S(1)} %collective-permute-done.6) | copy-start | bytes 196612
  47.0 18.3 %collective-permute-start.7 = (bf16[1,128,256]{2,1,0:T(8,128)(2,1)S(1)}, bf16[1,128,256]{2,1,0:T(8,128)(2,1)S(1)}, u32[]{:S(2)}, u32[]{:S(2)}) collective-permute-start(bf16[1,128,256]{2,1,0:T(8,128)(2,1)S(1)} %collective-permute-done.6), channel_id=1, source_target_pairs={{0,1},{1,2},{2,3},{3,4},{4,5},{5,6},{6,7},{7,8},{8,9},{9,10},{10,1... | collective-permute-start | bytes 196616 | tf_op jit(solution)/shard_map/ppermute | solution.py:96
  65.3 49.5 %copy-start.7 = (bf16[1,128,256]{2,1,0:T(8,128)(2,1)}, bf16[1,128,256]{2,1,0:T(8,128)(2,1)S(1)}, u32[]{:S(2)}) copy-start(bf16[1,128,256]{2,1,0:T(8,128)(2,1)S(1)} %collective-permute-done.7) | copy-start | bytes 196612
  65.3 6.5 %collective-permute-start.8 = (bf16[1,128,256]{2,1,0:T(8,128)(2,1)S(1)}, bf16[1,128,256]{2,1,0:T(8,128)(2,1)S(1)}, u32[]{:S(2)}, u32[]{:S(2)}) collective-permute-start(bf16[1,128,256]{2,1,0:T(8,128)(2,1)S(1)} %collective-permute-done.7), channel_id=1, source_target_pairs={{0,1},{1,2},{2,3},{3,4},{4,5},{5,6},{6,7},{7,8},{8,9},{9,10},{10,1... | collective-permute-start | bytes 196616 | tf_op jit(solution)/shard_map/ppermute | solution.py:96
  71.8 43.0 %copy-start.9 = (bf16[1,128,256]{2,1,0:T(8,128)(2,1)}, bf16[1,128,256]{2,1,0:T(8,128)(2,1)S(1)}, u32[]{:S(2)}) copy-start(bf16[1,128,256]{2,1,0:T(8,128)(2,1)S(1)} %collective-permute-done.8) | copy-start | bytes 196612
  71.8 6.4 %collective-permute-start.9 = (bf16[1,128,256]{2,1,0:T(8,128)(2,1)S(1)}, bf16[1,128,256]{2,1,0:T(8,128)(2,1)S(1)}, u32[]{:S(2)}, u32[]{:S(2)}) collective-permute-start(bf16[1,128,256]{2,1,0:T(8,128)(2,1)S(1)} %collective-permute-done.8), channel_id=1, source_target_pairs={{0,1},{1,2},{2,3},{3,4},{4,5},{5,6},{6,7},{7,8},{8,9},{9,10},{10,1... | collective-permute-start | bytes 196616 | tf_op jit(solution)/shard_map/ppermute | solution.py:96
  78.2 6.4 %collective-permute-start.10 = (bf16[1,128,256]{2,1,0:T(8,128)(2,1)S(1)}, bf16[1,128,256]{2,1,0:T(8,128)(2,1)S(1)}, u32[]{:S(2)}, u32[]{:S(2)}) collective-permute-start(bf16[1,128,256]{2,1,0:T(8,128)(2,1)S(1)} %collective-permute-done.9), channel_id=1, source_target_pairs={{0,1},{1,2},{2,3},{3,4},{4,5},{5,6},{6,7},{7,8},{8,9},{9,10},{10,1... | collective-permute-start | bytes 196616 | tf_op jit(solution)/shard_map/ppermute | solution.py:96
  84.6 6.4 %collective-permute-start.11 = (bf16[1,128,256]{2,1,0:T(8,128)(2,1)S(1)}, bf16[1,128,256]{2,1,0:T(8,128)(2,1)}, u32[]{:S(2)}, u32[]{:S(2)}) collective-permute-start(bf16[1,128,256]{2,1,0:T(8,128)(2,1)S(1)} %collective-permute-done.10), channel_id=1, source_target_pairs={{0,1},{1,2},{2,3},{3,4},{4,5},{5,6},{6,7},{7,8},{8,9},{9,10},{10,1... | collective-permute-start | bytes 196616 | tf_op jit(solution)/shard_map/ppermute | solution.py:96
  91.0 6.8 %collective-permute-start.12 = (bf16[1,128,256]{2,1,0:T(8,128)(2,1)}, bf16[1,128,256]{2,1,0:T(8,128)(2,1)}, u32[]{:S(2)}, u32[]{:S(2)}) collective-permute-start(bf16[1,128,256]{2,1,0:T(8,128)(2,1)} %collective-permute-done.11), channel_id=1, source_target_pairs={{0,1},{1,2},{2,3},{3,4},{4,5},{5,6},{6,7},{7,8},{8,9},{9,10},{10,1... | collective-permute-start | bytes 196616 | tf_op jit(solution)/shard_map/ppermute | solution.py:96
  97.8 6.7 %collective-permute-start.13 = (bf16[1,128,256]{2,1,0:T(8,128)(2,1)}, bf16[1,128,256]{2,1,0:T(8,128)(2,1)}, u32[]{:S(2)}, u32[]{:S(2)}) collective-permute-start(bf16[1,128,256]{2,1,0:T(8,128)(2,1)} %collective-permute-done.12), channel_id=1, source_target_pairs={{0,1},{1,2},{2,3},{3,4},{4,5},{5,6},{6,7},{7,8},{8,9},{9,10},{10,1... | collective-permute-start | bytes 196616 | tf_op jit(solution)/shard_map/ppermute | solution.py:96
  104.5 10.7 %collective-permute-start.14 = (bf16[1,128,256]{2,1,0:T(8,128)(2,1)}, bf16[1,128,256]{2,1,0:T(8,128)(2,1)}, u32[]{:S(2)}, u32[]{:S(2)}) collective-permute-start(bf16[1,128,256]{2,1,0:T(8,128)(2,1)} %collective-permute-done.13), channel_id=1, source_target_pairs={{0,1},{1,2},{2,3},{3,4},{4,5},{5,6},{6,7},{7,8},{8,9},{9,10},{10,1... | collective-permute-start | bytes 196616 | tf_op jit(solution)/shard_map/ppermute | solution.py:96
  (10 other events, 121.4 us)
